TPU v7x, 512 devices: a whole 4x8x8 slice. The times are simulated.
512 devices in a mesh: dom: 128 (over y, z, core), rep: 4 (over x).
Axes of the slice: x: 4, y: 8, z: 8, core: 2. Of those that a mesh axis runs over, the one named last changes fastest.
Arguments:
- feats: bfloat16 [131072, 256], P('dom'), may hold values from -6 to 6
- history: bfloat16 [131072, 256], P('dom'), may hold values from -6 to 6
- adj_inner: bfloat16 [131072, 1024], P('dom'), may hold values from -0.15625 to 0.15625
- adj_halo: bfloat16 [131072, 256], P('dom'), may hold values from -0.15625 to 0.15625
- halo_rows: int32 [16384, 2], P('dom'), may hold values from 0 to 1023
- w_self: bfloat16 [256, 256], replicated, may hold values from -0.375 to 0.375
- w_nbr: bfloat16 [256, 256], replicated, may hold values from -0.375 to 0.375
- b_enc: float32 [256], replicated, may hold values from -3 to 3
- edge_owner: int32 [131072, 2], P(('dom', 'rep')), may hold values from 0 to 127, all different within a row; in each aligned block of 256 rows (0 to 255, 256 to 511, ...) at most 8 rows name the same one
- edge_rows: int32 [131072, 2], P(('dom', 'rep')), may hold values from 0 to 1023
- labels: int32 [131072], P(('dom', 'rep')), may hold values 0 or 1
- w_dec1: bfloat16 [256, 256], replicated, may hold values from -0.375 to 0.375
- b_dec1: float32 [256], replicated, may hold values from -3 to 3
- w_dec2: bfloat16 [256], replicated, may hold values from -0.375 to 0.375
Outputs:
- embed: bfloat16 [131072, 256], P('dom')
- grad_embed: float32 [131072, 256], P(('dom', 'rep'))
- grad_dec1: float32 [256, 256], replicated
- grad_bias1: float32 [256], replicated
- grad_dec2: float32 [256], replicated
Inputs may be any that keep to these rules, and one draw needn't show every extreme that they name: `edge_owner`: among the rows of one device, no owner is named by more than 8 endpoints, a bound that some block reaches; the two endpoints of an edge have different owners.
All inputs are finite; a program needn't handle non-finite values. No bound on the sum of `labels` on one device may be relied on, other than what follows from the above.
Results may differ from a plain program's by a relative error of at most 0.0069.
Values may be sent and summed in bfloat16 or wider, within the bound.
A program may use at most 64 MiB of HBM per device.

v0:
```python
import jax
import jax.numpy as jnp
from jax import lax
from jax.sharding import PartitionSpec as P


def encode_block(rows_x, a_inner, a_halo, all_x, halo, w_self, w_nbr, b_enc):
    agg = (
        jnp.dot(a_inner, all_x, preferred_element_type=jnp.float32)
        + jnp.dot(a_halo, halo, preferred_element_type=jnp.float32)
    ).astype(jnp.bfloat16)
    pre = (
        jnp.dot(rows_x, w_self, preferred_element_type=jnp.float32)
        + jnp.dot(agg, w_nbr, preferred_element_type=jnp.float32)
        + b_enc
    )
    return jnp.maximum(pre, 0.0).astype(jnp.bfloat16)


def decode(head, tail, target, w_dec1, b_dec1, w_dec2):
    zprod = (head.astype(jnp.float32) * tail.astype(jnp.float32)).astype(jnp.bfloat16)
    pre = jnp.dot(zprod, w_dec1, preferred_element_type=jnp.float32) + b_dec1
    sig = jax.nn.sigmoid(pre)
    hidden = (pre * sig).astype(jnp.bfloat16)
    logit = jnp.dot(hidden, w_dec2, preferred_element_type=jnp.float32)
    dlogit = jax.nn.sigmoid(logit) - target
    d_pre = (
        dlogit[:, None] * w_dec2.astype(jnp.float32) * (sig * (1.0 + pre * (1.0 - sig)))
    ).astype(jnp.bfloat16)
    grad_w1 = jnp.dot(zprod.T, d_pre, preferred_element_type=jnp.float32)
    grad_b1 = jnp.sum(d_pre.astype(jnp.float32), axis=0)
    grad_w2 = jnp.sum(hidden.astype(jnp.float32) * dlogit[:, None], axis=0)
    dzval = jnp.dot(d_pre, w_dec1.T, preferred_element_type=jnp.float32)
    return (
        dzval * tail.astype(jnp.float32),
        dzval * head.astype(jnp.float32),
        grad_w1,
        grad_b1,
        grad_w2,
    )


def per_device(
    feats,
    history,
    adj_inner,
    adj_halo,
    halo_rows,
    w_self,
    w_nbr,
    b_enc,
    edge_owner,
    edge_rows,
    labels,
    w_dec1,
    b_dec1,
    w_dec2,
):
    n_dom = lax.axis_size("dom")
    nodes = feats.shape[0]
    width = feats.shape[1]
    halo = lax.all_to_all(
        history[lax.all_to_all(halo_rows, "dom", split_axis=0, concat_axis=0, tiled=True)],
        "dom",
        split_axis=0,
        concat_axis=0,
        tiled=True,
    ).reshape(-1, width)
    embed = encode_block(feats, adj_inner, adj_halo, feats, halo, w_self, w_nbr, b_enc)
    queries = edge_owner.shape[0]
    cap_edge = max(2, 4 * queries // n_dom)
    owners = edge_owner.reshape(-1)
    local = edge_rows.reshape(-1)
    match = (owners[:, None] == jnp.arange(n_dom, dtype=jnp.int32)[None, :]).astype(jnp.int32)
    slots = jnp.sum(jnp.cumsum(match, axis=0) * match, axis=1) - 1
    place = owners * cap_edge + slots
    send_ids = (
        jnp.zeros((n_dom * cap_edge,), jnp.int32).at[place].set(local).reshape(n_dom, cap_edge)
    )
    wanted = lax.all_to_all(send_ids, "dom", split_axis=0, concat_axis=0, tiled=True)
    fetched = lax.all_to_all(embed[wanted], "dom", split_axis=0, concat_axis=0, tiled=True)
    ends = fetched.reshape(-1, width)[place].reshape(queries, 2, width)
    target = labels.astype(jnp.float32)
    g_head, g_tail, gw1, gb1, gw2 = decode(ends[:, 0], ends[:, 1], target, w_dec1, b_dec1, w_dec2)
    grads = jnp.stack([g_head, g_tail], axis=1).reshape(-1, width)
    send_grads = jnp.zeros((n_dom * cap_edge, width), jnp.float32).at[place].set(grads)
    back = lax.all_to_all(
        send_grads.reshape(n_dom, cap_edge, width), "dom", split_axis=0, concat_axis=0, tiled=True
    )
    local_grad = (
        jnp.zeros((nodes, width), jnp.float32).at[wanted.reshape(-1)].add(back.reshape(-1, width))
    )
    grad_embed = lax.psum_scatter(local_grad, "rep", scatter_dimension=0, tiled=True)
    grad_dec1, grad_bias1, grad_dec2 = lax.psum((gw1, gb1, gw2), ("dom", "rep"))
    return (embed, grad_embed, grad_dec1, grad_bias1, grad_dec2)


def solution(mesh):
    placed = (
        P("dom", None),
        P("dom", None),
        P("dom", None),
        P("dom", None),
        P("dom", None),
        P(),
        P(),
        P(),
        P(("dom", "rep"), None),
        P(("dom", "rep"), None),
        P(("dom", "rep")),
        P(),
        P(),
        P(),
    )
    return jax.shard_map(
        per_device,
        mesh=mesh,
        in_specs=placed,
        out_specs=(P("dom", None), P(("dom", "rep"), None), P(), P(), P()),
        check_vma=False,
    )
```

profile of v0, /device:TPU:23, one launch (start us, length us, event | category | flops | bytes accessed | tf_op | source)
XLA Modules:
  0.0 414.1 jit_solution(18180660561444571792)
XLA Ops:
  8.0 1.6 copy.30
  9.6 17.7 %all-to-all-start = ((s32[128,1,2]{2,1,0:T(1,128)}), s32[128,1,2]{2,1,0:T(1,128)S(1)}, u32[]{:S(2)}, u32[]{:S(2)}) async-start(s32[128,1,2]{2,1,0:T(1,128)} %bitcast), calls=%async_computation | async-start | bytes 131072 | tf_op jit(solution)/shard_map/all_to_all | solution.py:63
  27.3 0.7 broadcast_multiply_fusion
  27.9 0.8 copy.33
  28.8 0.1 eq.29
  28.9 0.1 eq.25
  29.1 0.1 copy.32
  29.2 0.1 mul.61
  29.3 0.1 copy.35
  29.5 0.2 fusion.14
  29.8 0.2 fusion.13
  30.1 1.7 fusion.21
  31.8 1.3 fusion.20
  33.1 0.1 copy.37
  33.3 0.1 reshape.223
  33.4 2.4 scatter_custom_fusion
  35.9 0.7 all_to_all.29
  36.6 0.4 all-to-all-done
  37.0 13.3 %all-to-all-start.2 = ((s32[128,1,8]{2,1,0:T(1,128)}), s32[128,1,8]{2,1,0:T(1,128)S(1)}, u32[]{:S(2)}, u32[]{:S(2)}) async-start(s32[128,1,8]{2,1,0:T(1,128)} %bitcast.8), calls=%async_computation.2 | async-start | bytes 131072 | tf_op jit(solution)/shard_map/all_to_all | solution.py:80
  50.4 0.1 reshape.197
  50.5 1.2 gather_fusion
  51.7 0.7 reshape.196
  52.4 7.7 %all-to-all-done.2 = s32[128,1,8]{2,1,0:T(1,128)S(1)} async-done(((s32[128,1,8]{2,1,0:T(1,128)}), s32[128,1,8]{2,1,0:T(1,128)S(1)}, u32[]{:S(2)}, u32[]{:S(2)}) %all-to-all-start.2) | async-done | bytes 4128 | tf_op jit(solution)/shard_map/all_to_all | solution.py:80
  60.1 7.5 %all-to-all-start.1 = ((bf16[128,2,256]{2,1,0:T(2,128)(2,1)}), bf16[128,2,256]{2,1,0:T(2,128)(2,1)S(1)}, u32[]{:S(2)}, u32[]{:S(2)}) async-start(bf16[128,2,256]{2,1,0:T(2,128)(2,1)} %reshape.196), calls=%async_computation.1 | async-start | bytes 262144 | tf_op jit(solution)/shard_map/all_to_all | solution.py:62
  67.8 11.0 %all-to-all-done.1 = bf16[128,2,256]{2,1,0:T(2,128)(2,1)S(1)} async-done(((bf16[128,2,256]{2,1,0:T(2,128)(2,1)}), bf16[128,2,256]{2,1,0:T(2,128)(2,1)S(1)}, u32[]{:S(2)}, u32[]{:S(2)}) %all-to-all-start.1) | async-done | bytes 131104 | tf_op jit(solution)/shard_map/all_to_all | solution.py:62
  78.8 2.2 fusion.3
  81.0 5.0 %gather_fusion.1 = bf16[1024,256]{1,0:T(8,128)(2,1)} fusion(bf16[1024,256]{1,0:T(8,128)(2,1)S(1)} %fusion.3, s32[1024]{0:T(1024)S(1)} %broadcast_clamp_fusion), kind=kCustom, calls=%fused_computation.1 | custom fusion | bytes 1052672 | tf_op jit(solution)/shard_map/gather | solution.py:81
  86.0 7.5 %all-to-all-start.3 = ((bf16[128,8,256]{2,1,0:T(8,128)(2,1)}), bf16[128,8,256]{2,1,0:T(8,128)(2,1)S(1)}, u32[]{:S(2)}, u32[]{:S(2)}) async-start(bf16[128,8,256]{2,1,0:T(8,128)(2,1)} %bitcast.11), calls=%async_computation.3 | async-start | bytes 1048576 | tf_op jit(solution)/shard_map/all_to_all | solution.py:81
  93.6 17.8 %all-to-all-done.3 = bf16[128,8,256]{2,1,0:T(8,128)(2,1)S(1)} async-done(((bf16[128,8,256]{2,1,0:T(8,128)(2,1)}), bf16[128,8,256]{2,1,0:T(8,128)(2,1)S(1)}, u32[]{:S(2)}, u32[]{:S(2)}) %all-to-all-start.3) | async-done | bytes 524320 | tf_op jit(solution)/shard_map/all_to_all | solution.py:81
  111.4 1.9 gather_fusion.2
  113.4 0.1 reshape.189
  113.5 0.4 fusion.19
  114.0 0.2 multiply_convert_fusion.1
  114.2 0.1 fusion.22
  114.4 0.2 convert_reduce_fusion
  114.6 0.2 fusion.12
  114.8 0.4 copy.41
  115.3 0.4 reshape.231
  115.6 3.2 scatter_custom_fusion.1
  118.9 8.8 %all-to-all-start.4 = ((f32[128,8,256]{2,1,0:T(8,128)}), f32[128,8,256]{2,1,0:T(8,128)S(1)}, u32[]{:S(2)}, u32[]{:S(2)}) async-start(f32[128,8,256]{2,1,0:T(8,128)} %bitcast.73), calls=%async_computation.4 | async-start | bytes 2097152 | tf_op jit(solution)/shard_map/all_to_all | solution.py:87
  127.8 0.5 broadcast.156
  128.3 0.8 reduce.3
  129.2 0.9 fusion.23
  130.2 26.3 %all-to-all-done.4 = f32[128,8,256]{2,1,0:T(8,128)S(1)} async-done(((f32[128,8,256]{2,1,0:T(8,128)}), f32[128,8,256]{2,1,0:T(8,128)S(1)}, u32[]{:S(2)}, u32[]{:S(2)}) %all-to-all-start.4) | async-done | bytes 1048608 | tf_op jit(solution)/shard_map/all_to_all | solution.py:87
  156.5 7.1 %scatter_custom_fusion.2 = f32[1024,256]{1,0:T(8,128)} fusion(s32[1024]{0:T(1024)S(1)} %bitcast.84, f32[128,8,256]{2,1,0:T(8,128)S(1)} %all-to-all-done.4, f32[]{:T(128)} %constant.8.clone.1), kind=kCustom, calls=%fused_computation.14 | custom fusion | flops 262144 | bytes 2097156 | tf_op jit(solution)/shard_map/scatter-add | solution.py:91
  163.6 95.2 %all-reduce = (f32[256]{0:T(256)}, f32[256]{0:T(256)}) all-reduce(f32[256]{0:T(256)S(1)} %get-tuple-element.7, f32[256]{0:T(256)S(1)} %get-tuple-element.13), channel_id=1, replica_groups=mesh['dom'=128,'rep'=4] {'dom','rep'}, use_global_device_ids=true, to_apply=%region_9.10 | all-reduce | flops 512 | bytes 4096 | tf_op jit(solution)/shard_map/psum | solution.py:94
  258.9 146.1 %all-reduce.3.cloned.1.call-done = f32[256,256]{1,0:T(8,128)} async-done(((f32[256,256]{1,0:T(8,128)}), f32[256,256]{1,0:T(8,128)}) %all-reduce.3.cloned.1.call-update) | async-done | bytes 262160 | tf_op jit(solution)/shard_map/psum | solution.py:94
  404.9 1.7 copy.56
  (53 shorter events, 0.7 us)
Async XLA Ops:
  8.0 22.0 %copy-start = (bf16[1024,1024]{1,0:T(8,128)(2,1)S(1)}, bf16[1024,1024]{1,0:T(8,128)(2,1)}, u32[]{:S(2)}) copy-start(bf16[1024,1024]{1,0:T(8,128)(2,1)} %param.16) | copy-start | bytes 6291460
  8.0 22.0 %copy-start.4 = (bf16[1024,256]{1,0:T(8,128)(2,1)S(1)}, bf16[1024,256]{1,0:T(8,128)(2,1)}, u32[]{:S(2)}) copy-start(bf16[1024,256]{1,0:T(8,128)(2,1)} %param.14) | copy-start | bytes 1572868
  9.6 27.4 %all-to-all-start = ((s32[128,1,2]{2,1,0:T(1,128)}), s32[128,1,2]{2,1,0:T(1,128)S(1)}, u32[]{:S(2)}, u32[]{:S(2)}) async-start(s32[128,1,2]{2,1,0:T(1,128)} %bitcast), calls=%async_computation | async-start | bytes 131072 | tf_op jit(solution)/shard_map/all_to_all | solution.py:63
  30.0 1.8 copy-start.5
  30.1 1.8 copy-start.6
  30.1 3.1 copy-start.8
  31.8 18.7 %copy-start.2 = (bf16[1024,256]{1,0:T(8,128)(2,1)S(1)}, bf16[1024,256]{1,0:T(8,128)(2,1)}, u32[]{:S(2)}) copy-start(bf16[1024,256]{1,0:T(8,128)(2,1)} %param.15) | copy-start | bytes 1572868
  31.8 47.0 %copy-start.3 = (bf16[1024,256]{1,0:T(8,128)(2,1)S(1)}, bf16[1024,256]{1,0:T(8,128)(2,1)}, u32[]{:S(2)}) copy-start(bf16[1024,256]{1,0:T(8,128)(2,1)} %param.17) | copy-start | bytes 1572868
  31.8 47.0 %copy-start.9 = (f32[256]{0:T(256)S(1)}, f32[256]{0:T(256)}, u32[]{:S(2)}) copy-start(f32[256]{0:T(256)} %param.21) | copy-start | bytes 3076
  37.0 23.1 %all-to-all-start.2 = ((s32[128,1,8]{2,1,0:T(1,128)}), s32[128,1,8]{2,1,0:T(1,128)S(1)}, u32[]{:S(2)}, u32[]{:S(2)}) async-start(s32[128,1,8]{2,1,0:T(1,128)} %bitcast.8), calls=%async_computation.2 | async-start | bytes 131072 | tf_op jit(solution)/shard_map/all_to_all | solution.py:80
  60.1 18.7 %all-to-all-start.1 = ((bf16[128,2,256]{2,1,0:T(2,128)(2,1)}), bf16[128,2,256]{2,1,0:T(2,128)(2,1)S(1)}, u32[]{:S(2)}, u32[]{:S(2)}) async-start(bf16[128,2,256]{2,1,0:T(2,128)(2,1)} %reshape.196), calls=%async_computation.1 | async-start | bytes 262144 | tf_op jit(solution)/shard_map/all_to_all | solution.py:62
  81.0 5.0 %copy-start.1 = (bf16[1024,256]{1,0:T(8,128)(2,1)}, bf16[1024,256]{1,0:T(8,128)(2,1)S(1)}, u32[]{:S(2)}) copy-start(bf16[1024,256]{1,0:T(8,128)(2,1)S(1)} %fusion.3) | copy-start | bytes 1572868
  81.0 12.5 %copy-start.12 = (bf16[256]{0:T(256)(128)(2,1)S(1)}, bf16[256]{0:T(256)(128)(2,1)}, u32[]{:S(2)}) copy-start(bf16[256]{0:T(256)(128)(2,1)} %param.27) | copy-start | bytes 1540
  86.0 25.4 %all-to-all-start.3 = ((bf16[128,8,256]{2,1,0:T(8,128)(2,1)}), bf16[128,8,256]{2,1,0:T(8,128)(2,1)S(1)}, u32[]{:S(2)}, u32[]{:S(2)}) async-start(bf16[128,8,256]{2,1,0:T(8,128)(2,1)} %bitcast.11), calls=%async_computation.3 | async-start | bytes 1048576 | tf_op jit(solution)/shard_map/all_to_all | solution.py:81
  111.4 2.5 copy-start.7
  111.4 2.5 copy-start.11
  113.4 1.0 copy-start.10
  118.9 37.6 %all-to-all-start.4 = ((f32[128,8,256]{2,1,0:T(8,128)}), f32[128,8,256]{2,1,0:T(8,128)S(1)}, u32[]{:S(2)}, u32[]{:S(2)}) async-start(f32[128,8,256]{2,1,0:T(8,128)} %bitcast.73), calls=%async_computation.4 | async-start | bytes 2097152 | tf_op jit(solution)/shard_map/all_to_all | solution.py:87
  127.7 277.2 %all-reduce.3.cloned.1.call-start = ((), (), s32[]{:S(2)}) async-start(), calls=%async_computation.7 | async-start | bytes 524288 | tf_op jit(solution)/shard_map/psum | solution.py:94
  130.2 274.8 %reduce-scatter.2.cloned.1.call-start = ((), (), s32[]{:S(2)}) async-start(), calls=%async_computation.6 | async-start | bytes 1310720 | tf_op jit(solution)/shard_map/reduce_scatter | solution.py:93
Sparse Core Ops, SparseCore 0:
  134.9 269.9 all-reduce.2
Sparse Core Ops, SparseCore 1:
  163.7 20.9 reduce-scatter.1
where the time goes:
time: 415 us; the launch traced here: 414 us
  waiting for transfers between devices  209 us (50%)
  blocking collectives  95.2 us (23%)
  starting transfers between devices  55 us (13%)
  local copies, waits for them, and re-layouts  22.4 us (5%)
  between operations  15.9 us (4%)
  other arithmetic  9.45 us (2%)
  matrix products  6.74 us (2%)
    psum x1, waiting for transfers between devices, per_device(): grad_dec1, grad_bias1, grad_dec2 = lax.psum((gw1, gb1, gw2), ('dom', 'rep'))  146 us
    psum x1, blocking collectives, per_device(): grad_dec1, grad_bias1, grad_dec2 = lax.psum((gw1, gb1, gw2), ('dom', 'rep'))  95.2 us
    all_to_all x1, waiting for transfers between devices, per_device(): lax.all_to_all(send_grads.reshape(n_dom, cap_edge, width), 'dom', split_a...  26.3 us
    all_to_all x1, waiting for transfers between devices, per_device(): lax.all_to_all(embed[wanted], 'dom', split_axis=0, concat_axis=0, tiled=T...  17.8 us
    all_to_all x1, starting transfers between devices, per_device(): lax.all_to_all(halo_rows, 'dom', split_axis=0, concat_axis=0, tiled=True)  17.7 us
    all_to_all x1, starting transfers between devices, per_device(): lax.all_to_all(send_ids, 'dom', split_axis=0, concat_axis=0, tiled=True)  13.3 us
    all_to_all x1, waiting for transfers between devices, per_device(): lax.all_to_all(history[lax.all_to_all(halo_rows, 'dom', split_axis=0, con...  11 us
    all_to_all x1, starting transfers between devices, per_device(): lax.all_to_all(send_grads.reshape(n_dom, cap_edge, width), 'dom', split_a...  8.84 us
  transfers between devices with their start and end apart: 7, of which 6 were waited for; matrix products, arithmetic and copies ran while one was open for 5% of the time, Pallas kernels for 0%

commit v1 on v0

--- a/solution.py
+++ b/solution.py
@@ -91,7 +91,7 @@
         jnp.zeros((nodes, width), jnp.float32).at[wanted.reshape(-1)].add(back.reshape(-1, width))
     )
     grad_embed = lax.psum_scatter(local_grad, "rep", scatter_dimension=0, tiled=True)
-    grad_dec1, grad_bias1, grad_dec2 = lax.psum((gw1, gb1, gw2), ("dom", "rep"))
+    grad_dec1, grad_bias1, grad_dec2 = lax.psum(lax.psum((gw1, gb1, gw2), "rep"), "dom")
     return (embed, grad_embed, grad_dec1, grad_bias1, grad_dec2)
 
 

time: 415 us -> 459 us (1.11)
  the two profiles are of different devices: /device:TPU:23 before, /device:TPU:1 now
where the time goes in v1:
time: 459 us; the launch traced here: 458 us
  blocking collectives  260 us (57%)
  waiting for transfers between devices  95.7 us (21%)
  starting transfers between devices  49.4 us (11%)
  local copies, waits for them, and re-layouts  22.4 us (5%)
  between operations  14.2 us (3%)
  other arithmetic  9.46 us (2%)
  matrix products  6.74 us (1%)
    psum x1, blocking collectives, per_device(): lax.psum(lax.psum((gw1, gb1, gw2), 'rep'), 'dom')  253 us
    psum x1, waiting for transfers between devices, per_device(): lax.psum((gw1, gb1, gw2), 'rep')  52.4 us
    all_to_all x1, waiting for transfers between devices, per_device(): lax.all_to_all(embed[wanted], 'dom', split_axis=0, concat_axis=0, tiled=T...  19.5 us
    all_to_all x1, starting transfers between devices, per_device(): lax.all_to_all(halo_rows, 'dom', split_axis=0, concat_axis=0, tiled=True)  18.4 us
    all_to_all x1, waiting for transfers between devices, per_device(): lax.all_to_all(history[lax.all_to_all(halo_rows, 'dom', split_axis=0, con...  12.2 us
    all_to_all x1, starting transfers between devices, per_device(): lax.all_to_all(send_ids, 'dom', split_axis=0, concat_axis=0, tiled=True)  11.6 us
    all_to_all x1, waiting for transfers between devices, per_device(): lax.all_to_all(send_ids, 'dom', split_axis=0, concat_axis=0, tiled=True)  9.41 us
  transfers between devices with their start and end apart: 8, of which 5 were waited for; matrix products, arithmetic and copies ran while one was open for 4% of the time, Pallas kernels for 0%

profile of v1, /device:TPU:1, one launch (start us, length us, event | category | flops | bytes accessed | tf_op | source)
XLA Modules:
  0.0 458.1 jit_solution(6698185986009296410)
XLA Ops:
  7.2 1.6 copy.30
  8.8 18.4 %all-to-all-start = ((s32[128,1,2]{2,1,0:T(1,128)}), s32[128,1,2]{2,1,0:T(1,128)S(1)}, u32[]{:S(2)}, u32[]{:S(2)}) async-start(s32[128,1,2]{2,1,0:T(1,128)} %bitcast), calls=%async_computation | async-start | bytes 131072 | tf_op jit(solution)/shard_map/all_to_all | solution.py:63
  27.2 0.7 broadcast_multiply_fusion
  27.9 0.8 copy.33
  28.7 0.1 eq.29
  28.8 0.1 eq.25
  29.0 0.1 copy.32
  29.1 0.1 mul.61
  29.3 0.1 copy.35
  29.4 0.2 fusion.14
  29.7 0.2 fusion.13
  30.0 1.7 fusion.21
  31.8 1.3 fusion.20
  33.1 0.1 copy.37
  33.2 0.1 reshape.223
  33.4 2.4 scatter_custom_fusion
  35.8 0.7 all_to_all.29
  36.5 2.1 all-to-all-done
  38.6 11.6 %all-to-all-start.2 = ((s32[128,1,8]{2,1,0:T(1,128)}), s32[128,1,8]{2,1,0:T(1,128)S(1)}, u32[]{:S(2)}, u32[]{:S(2)}) async-start(s32[128,1,8]{2,1,0:T(1,128)} %bitcast.8), calls=%async_computation.2 | async-start | bytes 131072 | tf_op jit(solution)/shard_map/all_to_all | solution.py:80
  50.3 0.1 reshape.197
  50.4 1.2 gather_fusion
  51.6 0.7 reshape.196
  52.3 9.4 %all-to-all-done.2 = s32[128,1,8]{2,1,0:T(1,128)S(1)} async-done(((s32[128,1,8]{2,1,0:T(1,128)}), s32[128,1,8]{2,1,0:T(1,128)S(1)}, u32[]{:S(2)}, u32[]{:S(2)}) %all-to-all-start.2) | async-done | bytes 4128 | tf_op jit(solution)/shard_map/all_to_all | solution.py:80
  61.7 5.7 %all-to-all-start.1 = ((bf16[128,2,256]{2,1,0:T(2,128)(2,1)}), bf16[128,2,256]{2,1,0:T(2,128)(2,1)S(1)}, u32[]{:S(2)}, u32[]{:S(2)}) async-start(bf16[128,2,256]{2,1,0:T(2,128)(2,1)} %reshape.196), calls=%async_computation.1 | async-start | bytes 262144 | tf_op jit(solution)/shard_map/all_to_all | solution.py:62
  67.6 12.2 %all-to-all-done.1 = bf16[128,2,256]{2,1,0:T(2,128)(2,1)S(1)} async-done(((bf16[128,2,256]{2,1,0:T(2,128)(2,1)}), bf16[128,2,256]{2,1,0:T(2,128)(2,1)S(1)}, u32[]{:S(2)}, u32[]{:S(2)}) %all-to-all-start.1) | async-done | bytes 131104 | tf_op jit(solution)/shard_map/all_to_all | solution.py:62
  79.8 2.2 fusion.3
  82.0 4.9 %gather_fusion.1 = bf16[1024,256]{1,0:T(8,128)(2,1)} fusion(bf16[1024,256]{1,0:T(8,128)(2,1)S(1)} %fusion.3, s32[1024]{0:T(1024)S(1)} %broadcast_clamp_fusion), kind=kCustom, calls=%fused_computation.1 | custom fusion | bytes 1052672 | tf_op jit(solution)/shard_map/gather | solution.py:81
  87.0 6.4 %all-to-all-start.3 = ((bf16[128,8,256]{2,1,0:T(8,128)(2,1)}), bf16[128,8,256]{2,1,0:T(8,128)(2,1)S(1)}, u32[]{:S(2)}, u32[]{:S(2)}) async-start(bf16[128,8,256]{2,1,0:T(8,128)(2,1)} %bitcast.11), calls=%async_computation.3 | async-start | bytes 1048576 | tf_op jit(solution)/shard_map/all_to_all | solution.py:81
  93.4 19.5 %all-to-all-done.3 = bf16[128,8,256]{2,1,0:T(8,128)(2,1)S(1)} async-done(((bf16[128,8,256]{2,1,0:T(8,128)(2,1)}), bf16[128,8,256]{2,1,0:T(8,128)(2,1)S(1)}, u32[]{:S(2)}, u32[]{:S(2)}) %all-to-all-start.3) | async-done | bytes 524320 | tf_op jit(solution)/shard_map/all_to_all | solution.py:81
  113.0 1.9 gather_fusion.2
  114.9 0.1 reshape.189
  115.0 0.4 fusion.19
  115.5 0.2 multiply_convert_fusion.1
  115.7 0.1 fusion.22
  115.9 0.2 convert_reduce_fusion
  116.1 0.2 fusion.12
  116.4 0.4 copy.41
  116.8 0.4 reshape.231
  117.1 3.3 scatter_custom_fusion.1
  120.4 7.1 %all-to-all-start.4 = ((f32[128,8,256]{2,1,0:T(8,128)}), f32[128,8,256]{2,1,0:T(8,128)S(1)}, u32[]{:S(2)}, u32[]{:S(2)}) async-start(f32[128,8,256]{2,1,0:T(8,128)} %bitcast.73), calls=%async_computation.4 | async-start | bytes 2097152 | tf_op jit(solution)/shard_map/all_to_all | solution.py:87
  127.6 0.9 fusion.23
  128.6 0.5 broadcast.156
  129.1 0.8 reduce.3
  130.0 52.4 %all-reduce.5.cloned.1.call-done = f32[256,256]{1,0:T(8,128)} async-done(((f32[256,256]{1,0:T(8,128)}), f32[256,256]{1,0:T(8,128)}) %all-reduce.5.cloned.1.call-update) | async-done | bytes 262160 | tf_op jit(solution)/shard_map/psum | solution.py:94
  182.6 7.1 %scatter_custom_fusion.2 = f32[1024,256]{1,0:T(8,128)} fusion(s32[1024]{0:T(1024)S(1)} %bitcast.84, f32[128,8,256]{2,1,0:T(8,128)S(1)} %all-to-all-done.4, f32[]{:T(128)} %constant.8.clone.1), kind=kCustom, calls=%fused_computation.14 | custom fusion | flops 262144 | bytes 2097156 | tf_op jit(solution)/shard_map/scatter-add | solution.py:91
  189.7 7.6 %all-reduce.1 = (f32[256]{0:T(256)S(1)}, f32[256]{0:T(256)S(1)}) all-reduce(f32[256]{0:T(256)S(1)} %get-tuple-element.9, f32[256]{0:T(256)S(1)} %get-tuple-element.15), channel_id=1, replica_groups=mesh['dom'=128,'rep'=4] {'rep'}, use_global_device_ids=true, to_apply=%region_10.11 | all-reduce | flops 512 | bytes 4096 | tf_op jit(solution)/shard_map/psum | solution.py:94
  197.3 252.6 %all-reduce = (f32[256]{0:T(256)}, f32[256]{0:T(256)}) all-reduce(f32[256]{0:T(256)S(1)} %get-tuple-element.7, f32[256]{0:T(256)S(1)} %get-tuple-element.8), channel_id=1, replica_groups=mesh['dom'=128,'rep'=4] {'dom'}, use_global_device_ids=true, to_apply=%region_11.12 | all-reduce | flops 512 | bytes 4096 | tf_op jit(solution)/shard_map/psum | solution.py:94
  449.9 1.7 copy.57
  (57 shorter events, 0.8 us)
Async XLA Ops:
  7.2 22.8 %copy-start = (bf16[1024,1024]{1,0:T(8,128)(2,1)S(1)}, bf16[1024,1024]{1,0:T(8,128)(2,1)}, u32[]{:S(2)}) copy-start(bf16[1024,1024]{1,0:T(8,128)(2,1)} %param.16) | copy-start | bytes 6291460
  7.2 22.8 %copy-start.4 = (bf16[1024,256]{1,0:T(8,128)(2,1)S(1)}, bf16[1024,256]{1,0:T(8,128)(2,1)}, u32[]{:S(2)}) copy-start(bf16[1024,256]{1,0:T(8,128)(2,1)} %param.14) | copy-start | bytes 1572868
  8.8 29.9 %all-to-all-start = ((s32[128,1,2]{2,1,0:T(1,128)}), s32[128,1,2]{2,1,0:T(1,128)S(1)}, u32[]{:S(2)}, u32[]{:S(2)}) async-start(s32[128,1,2]{2,1,0:T(1,128)} %bitcast), calls=%async_computation | async-start | bytes 131072 | tf_op jit(solution)/shard_map/all_to_all | solution.py:63
  30.0 1.8 copy-start.5
  30.0 1.8 copy-start.6
  30.0 3.1 copy-start.8
  31.7 18.7 %copy-start.2 = (bf16[1024,256]{1,0:T(8,128)(2,1)S(1)}, bf16[1024,256]{1,0:T(8,128)(2,1)}, u32[]{:S(2)}) copy-start(bf16[1024,256]{1,0:T(8,128)(2,1)} %param.15) | copy-start | bytes 1572868
  31.8 48.1 %copy-start.3 = (bf16[1024,256]{1,0:T(8,128)(2,1)S(1)}, bf16[1024,256]{1,0:T(8,128)(2,1)}, u32[]{:S(2)}) copy-start(bf16[1024,256]{1,0:T(8,128)(2,1)} %param.17) | copy-start | bytes 1572868
  31.8 48.1 %copy-start.9 = (f32[256]{0:T(256)S(1)}, f32[256]{0:T(256)}, u32[]{:S(2)}) copy-start(f32[256]{0:T(256)} %param.21) | copy-start | bytes 3076
  38.6 23.1 %all-to-all-start.2 = ((s32[128,1,8]{2,1,0:T(1,128)}), s32[128,1,8]{2,1,0:T(1,128)S(1)}, u32[]{:S(2)}, u32[]{:S(2)}) async-start(s32[128,1,8]{2,1,0:T(1,128)} %bitcast.8), calls=%async_computation.2 | async-start | bytes 131072 | tf_op jit(solution)/shard_map/all_to_all | solution.py:80
  61.7 18.0 %all-to-all-start.1 = ((bf16[128,2,256]{2,1,0:T(2,128)(2,1)}), bf16[128,2,256]{2,1,0:T(2,128)(2,1)S(1)}, u32[]{:S(2)}, u32[]{:S(2)}) async-start(bf16[128,2,256]{2,1,0:T(2,128)(2,1)} %reshape.196), calls=%async_computation.1 | async-start | bytes 262144 | tf_op jit(solution)/shard_map/all_to_all | solution.py:62
  82.0 5.0 %copy-start.1 = (bf16[1024,256]{1,0:T(8,128)(2,1)}, bf16[1024,256]{1,0:T(8,128)(2,1)S(1)}, u32[]{:S(2)}) copy-start(bf16[1024,256]{1,0:T(8,128)(2,1)S(1)} %fusion.3) | copy-start | bytes 1572868
  82.0 11.4 %copy-start.12 = (bf16[256]{0:T(256)(128)(2,1)S(1)}, bf16[256]{0:T(256)(128)(2,1)}, u32[]{:S(2)}) copy-start(bf16[256]{0:T(256)(128)(2,1)} %param.27) | copy-start | bytes 1540
  87.0 26.0 %all-to-all-start.3 = ((bf16[128,8,256]{2,1,0:T(8,128)(2,1)}), bf16[128,8,256]{2,1,0:T(8,128)(2,1)S(1)}, u32[]{:S(2)}, u32[]{:S(2)}) async-start(bf16[128,8,256]{2,1,0:T(8,128)(2,1)} %bitcast.11), calls=%async_computation.3 | async-start | bytes 1048576 | tf_op jit(solution)/shard_map/all_to_all | solution.py:81
  113.0 2.5 copy-start.7
  113.0 2.5 copy-start.11
  114.9 1.0 copy-start.10
  120.4 62.1 %all-to-all-start.4 = ((f32[128,8,256]{2,1,0:T(8,128)}), f32[128,8,256]{2,1,0:T(8,128)S(1)}, u32[]{:S(2)}, u32[]{:S(2)}) async-start(f32[128,8,256]{2,1,0:T(8,128)} %bitcast.73), calls=%async_computation.4 | async-start | bytes 2097152 | tf_op jit(solution)/shard_map/all_to_all | solution.py:87
  127.5 54.9 %all-reduce.5.cloned.1.call-start = ((), (), s32[]{:S(2)}) async-start(), calls=%async_computation.7 | async-start | bytes 524288 | tf_op jit(solution)/shard_map/psum | solution.py:94
  128.6 321.3 %all-reduce.7.cloned.1.call-start = ((), (), s32[]{:S(2)}) async-start(), calls=%async_computation.8 | async-start | bytes 524288 | tf_op jit(solution)/shard_map/psum | solution.py:94
  182.5 267.4 %reduce-scatter.2.cloned.1.call-start = ((), (), s32[]{:S(2)}) async-start(), calls=%async_computation.6 | async-start | bytes 1310720 | tf_op jit(solution)/shard_map/reduce_scatter | solution.py:93
Sparse Core Ops, SparseCore 0:
  131.3 51.1 all-reduce.4
  186.0 191.5 all-reduce.6
  381.3 25.3 reduce-scatter.1
